TPU v7x, 32 devices: a whole 2x2x4 slice. The times are simulated.
32 devices in a mesh: group: 16 (over z, y, core), tp: 2 (over x).
Axes of the slice: x: 2, y: 2, z: 4, core: 2. Of those that a mesh axis runs over, the one named last changes fastest.
Arguments:
- tokens: bfloat16 [8192, 3200], P('group', 'tp'), may hold values from -6 to 6
- norm_gain: bfloat16 [3200], P('tp'), may hold values from 0.25 to 1.75
- w_qkv: bfloat16 [3200, 3, 2048], P('group', None, 'tp'), may hold values from -1 to 1, as said below
- qk_gain: float32 [2, 2048], P(None, 'tp'), may hold values from 0.5 to 8
- w_out: bfloat16 [2048, 3200], P('tp', 'group'), may hold values from -0.125 to 0.125
- layer_scale: float32 [3200], P('tp'), may hold values from 0.3 to 1.5
- request: int32 [8192], P('group'), may hold values from 0 to 8191, as said below
- owner: int32 [8192, 1], P('group'), may hold values from 0 to 15; in each aligned block of 512 rows (0 to 511, 512 to 1023, ...) at most 64 rows name the same one
Outputs:
- routed: bfloat16 [16, 16, 64, 3200], P('group', None, None, 'tp')
Inputs may be any that keep to these rules, and one draw needn't show every extreme that they name: Requests never cross a block of 1024 rows starting at a multiple of 1024, and blocks share none; in each such block exactly one request holds rows on both sides of its middle, at most 128 on each side, exactly 128 on each side in the first block; the first row's number is 0 and the last row's is 8191. Among one group's 512 rows at most 64 name the same owner; some owner is named by exactly 64 rows of some group. `w_qkv`: column scales of the projections vary across the columns.
All inputs are finite; a program needn't handle non-finite values.
Results may differ from a plain program's by a relative error of at most 0.0117.
The roundings to bfloat16 on the way count: a program that leaves them out, or rounds other values in their place, can miss the bound.
Values may be sent and summed in bfloat16 or wider, within the bound.
A program may use at most 128 MiB of HBM per device.

v0:
```python
import math
import jax
import jax.numpy as jnp
from jax import lax
from jax.sharding import PartitionSpec as P

HD = 128
SHARE = 128


def swapped(value, axis, apart):
    mask = 2**apart
    pairs = [(source, source ^ mask) for source in range(lax.axis_size(axis))]
    return lax.ppermute(value, axis, pairs)


def from_next(value, axis):
    count = lax.axis_size(axis)
    return lax.ppermute(value, axis, [((i + 1) % count, i) for i in range(count)])


def shards(tokens, norm_gain, w_qkv, qk_gain, w_out, layer_scale, request, owner):
    rows, feat_local = tokens.shape
    tp_count = lax.axis_size("tp")
    group_count = lax.axis_size("group")
    local_width = w_qkv.shape[2]
    head_count = local_width // HD
    me_tp = lax.axis_index("tp")
    w_all = lax.all_gather(
        w_qkv.reshape(w_qkv.shape[0], 3 * local_width), "group", axis=0, tiled=True
    )
    whole = jnp.zeros((rows, feat_local * tp_count), jnp.bfloat16)
    gain_all = jnp.zeros((1, feat_local * tp_count), jnp.bfloat16)
    piece, gain = (tokens, norm_gain.reshape(1, feat_local))
    for step in range(tp_count):
        at = (me_tp + step) % tp_count * feat_local
        whole = lax.dynamic_update_slice(whole, piece, (0, at))
        gain_all = lax.dynamic_update_slice(gain_all, gain, (0, at))
        if step < tp_count - 1:
            piece, gain = (from_next(piece, "tp"), from_next(gain, "tp"))
    whole, late_out = lax.optimization_barrier((whole, w_out))
    per = group_count // tp_count
    pairs = []
    for g in range(group_count):
        for b in range(tp_count):
            t, j = (g // per, g % per)
            to_g = (b - t) % tp_count * per + j
            pairs.append((g * tp_count + b, to_g * tp_count + t))
    w_piece = lax.ppermute(late_out.T, ("group", "tp"), pairs)
    w_o = lax.all_gather(w_piece, "group", axis=0, tiled=True)
    w_o = w_o.reshape(tp_count, feat_local, local_width)
    xwide = whole.astype(jnp.float32)
    stat = jnp.mean(xwide * xwide, axis=-1, keepdims=True)
    normed = (xwide * lax.rsqrt(stat + 1e-06) * gain_all.astype(jnp.float32)).astype(jnp.bfloat16)
    qkv = jnp.dot(normed, w_all, preferred_element_type=jnp.float32)
    query = qkv[:, :local_width]
    key_rows = qkv[:, local_width : 2 * local_width]
    value = qkv[:, 2 * local_width :].astype(jnp.bfloat16)
    qsum, ksum = lax.psum(
        (jnp.sum(query * query, axis=-1), jnp.sum(key_rows * key_rows, axis=-1)), "tp"
    )
    total_width = local_width * tp_count
    qnorm = (query * lax.rsqrt(qsum / total_width + 1e-06)[:, None] * qk_gain[0]).astype(
        jnp.bfloat16
    )
    knorm = (key_rows * lax.rsqrt(ksum / total_width + 1e-06)[:, None] * qk_gain[1]).astype(
        jnp.bfloat16
    )
    parity = lax.axis_index("group") % 2
    seam = jnp.where(parity == 0, rows - SHARE, 0).astype(jnp.int32)
    key_window = lax.dynamic_slice_in_dim(knorm, seam, SHARE, 0)
    id_window = lax.dynamic_slice_in_dim(request, seam, SHARE, 0)
    paired_key, paired_ids = swapped((key_window, id_window), "group", 0)
    all_keys = jnp.concatenate([knorm, paired_key], axis=0)
    all_ids = jnp.concatenate([request, paired_ids], axis=0)
    qheads = qnorm.reshape(rows, head_count, HD)
    kheads = all_keys.reshape(rows + SHARE, head_count, HD)
    scores = jnp.einsum(
        "qhd,khd->hqk", qheads, kheads, preferred_element_type=jnp.float32
    ) / math.sqrt(HD)
    same = request[:, None] == all_ids[None, :]
    scores = jnp.where(same[None], scores, -jnp.inf)
    top = jnp.max(scores, axis=-1, keepdims=True)
    expo = jnp.exp(scores - top)
    probs = (expo / jnp.sum(expo, axis=-1, keepdims=True)).astype(jnp.bfloat16)
    value_window = lax.dynamic_slice_in_dim(value, seam, SHARE, 0)
    all_values = jnp.concatenate([value, swapped(value_window, "group", 0)], axis=0)
    vheads = all_values.reshape(rows + SHARE, head_count, HD)
    attended = jnp.einsum("hqk,khd->qhd", probs, vheads, preferred_element_type=jnp.float32)
    attended = attended.astype(jnp.bfloat16).reshape(rows, local_width)
    branch = jnp.zeros((rows, feat_local), jnp.float32)
    for step in range(tp_count):
        onward = from_next(attended, "tp") if step < tp_count - 1 else None
        part = lax.dot_general(
            attended, w_o[step], (((1,), (1,)), ((), ())), preferred_element_type=jnp.float32
        )
        branch = branch + part.astype(jnp.bfloat16).astype(jnp.float32)
        attended = onward
    mixed = (tokens.astype(jnp.float32) + layer_scale * branch).astype(jnp.bfloat16)
    capacity = max(2, 2 * rows // group_count)
    target = owner[:, 0]
    onehot = (target[:, None] == jnp.arange(group_count, dtype=jnp.int32)[None, :]).astype(
        jnp.int32
    )
    slot = jnp.sum((jnp.cumsum(onehot, axis=0) - onehot) * onehot, axis=-1)
    place = target * capacity + slot
    select = (
        jnp.arange(group_count * capacity, dtype=jnp.int32)[:, None] == place[None, :]
    ).astype(jnp.bfloat16)
    outbox = jnp.dot(select, mixed, preferred_element_type=jnp.float32).astype(jnp.bfloat16)
    outbox = outbox.reshape(group_count, capacity, feat_local)
    inbox = lax.all_to_all(outbox, "group", split_axis=0, concat_axis=0, tiled=True)
    return inbox[None]


def solution(mesh):
    in_specs = (
        P("group", "tp"),
        P("tp"),
        P("group", None, "tp"),
        P(None, "tp"),
        P("tp", "group"),
        P("tp"),
        P("group"),
        P("group", None),
    )
    out_specs = P("group", None, None, "tp")
    return jax.shard_map(shards, mesh=mesh, in_specs=in_specs, out_specs=out_specs, check_vma=False)
```

profile of v0, /device:TPU:1, one launch (start us, length us, event | category | flops | bytes accessed | tf_op | source)
XLA Modules:
  0.0 316.9 jit_solution(11441685035728626753)
XLA Ops:
  6.5 0.0 all-gather.3.cloned.1.call-start
  6.5 2.4 copy.23
  8.9 0.0 all-gather.3.cloned.1.call-update
  9.0 0.0 all-gather.5.cloned.1.call-start
  9.0 2.1 collective-permute-start
  11.1 0.2 broadcast_in_dim.16
  11.3 0.0 copy-start.8
  11.3 0.0 copy-start.5
  11.4 0.0 copy-start.6
  11.4 0.0 copy-start.7
  11.4 1.6 constant_dynamic-update-slice_fusion.1
  13.0 33.9 %collective-permute-done = bf16[512,1600]{0,1:T(8,128)(2,1)} collective-permute-done((bf16[512,1600]{0,1:T(8,128)(2,1)}, bf16[512,1600]{0,1:T(8,128)(2,1)}, u32[]{:S(2)}, u32[]{:S(2)}) %collective-permute-start) | collective-permute-done | bytes 1638432 | tf_op jit(solution)/shard_map/ppermute | solution.py:19
  47.0 1.6 constant_dynamic-update-slice_fusion
  48.6 0.0 copy-done.8
  48.6 1.4 collective-permute-start.5
  50.0 0.0 collective-permute-done.5
  50.0 0.0 all-gather.5.cloned.1.call-update
  50.0 0.0 copy-done.5
  50.1 31.1 %collective-permute-start.1 = (bf16[1,1600]{1,0:T(2,128)(2,1)S(1)}, bf16[1,1600]{1,0:T(2,128)(2,1)S(1)}, u32[]{:S(2)}, u32[]{:S(2)}) collective-permute-start(bf16[1,1600]{1,0:T(2,128)(2,1)S(1)} %reshape.96), channel_id=1, source_target_pairs={{1,0},{0,1},{3,2},{2,3},{5,4},{4,5},{7,6},{6,7},{9,8},{8,9},{11,10... | collective-permute-start | bytes 9608 | tf_op jit(solution)/shard_map/ppermute | solution.py:19
  81.2 0.0 copy-done.6
  81.2 0.1 dynamic_slice.10
  81.3 2.3 collective-permute-start.3
  83.6 0.0 copy-done.7
  83.6 0.3 dynamic_update_slice.16
  83.9 0.5 collective-permute-done.3
  84.4 0.0 collective-permute-done.1
  84.5 0.3 dynamic_update_slice.17
  84.8 0.8 fusion.2
  85.5 28.8 %all-gather.3.cloned.1.call-done = bf16[3200,3072]{1,0:T(8,128)(2,1)} async-done(((bf16[200,3072]{1,0:T(8,128)(2,1)}), bf16[3200,3072]{1,0:T(8,128)(2,1)}) %all-gather.3.cloned.1.call-update) | async-done | bytes 19660816 | tf_op jit(solution)/shard_map/all_gather | solution.py:29
  114.3 14.3 %fusion.9 = f32[512,3072]{1,0:T(8,128)S(1)} fusion(bf16[3200,3072]{1,0:T(8,128)(2,1)} %all-gather.3.cloned.1.call-done, bf16[512,3200]{0,1:T(8,128)(2,1)S(1)} %constant_dynamic-update-slice_fusion, f32[3200]{0:T(1024)S(1)} %mul.106, f32[512]{0:T(512)S(1)} %add_rsqrt_fusion.2), kind=kOutput, calls=%fused_computation.15 | convolution fusion | flops 10072883200 | bytes 29243904 | tf_op jit(solution)/shard_map/dot_general | solution.py:55
  128.6 0.0 copy-start
  128.6 0.2 slice.65
  128.8 0.3 collective-permute-start.2
  129.1 0.3 multiply_reduce_fusion.1
  129.5 1.8 copy-done
  131.3 14.3 %all-reduce = (f32[512]{0:T(512)S(1)}, f32[512]{0:T(512)S(1)}) all-reduce(f32[512]{0:T(512)S(1)} %get-tuple-element.10, f32[512]{0:T(512)S(1)} %get-tuple-element.9), channel_id=1, replica_groups=mesh['group'=16,'tp'=2] {'tp'}, use_global_device_ids=true, to_apply=%region_7.8 | all-reduce | flops 1024 | bytes 8192 | tf_op jit(solution)/shard_map/psum | solution.py:59
  145.6 3.7 %fusion.29 = (bf16[64,8,8,128]{3,2,1,0:T(8,128)(2,1)}, bf16[512,1024]{1,0:T(8,128)(2,1)S(1)}) fusion(f32[512,3072]{1,0:T(8,128)} %copy-done, f32[1024]{0:T(1024)S(1)} %bitcast.56, f32[512]{0:T(512)S(1)} %get-tuple-element.20, f32[1024]{0:T(1024)S(1)} %bitcast.57, f32[512]{0:T(512)S(1)} %get-tuple-element.19), kind=kLoop, calls=%fused_computation.37 | loop fusion | flops 3145728 | bytes 6303744
  149.3 0.7 constant_dynamic-slice_fusion
  150.0 0.7 collective-permute-start.4
  150.7 1.0 broadcast_compare_fusion
  151.7 0.0 collective-permute-done.2
  151.7 1.0 pad_maximum_fusion
  152.8 0.0 copy-start.1
  152.8 1.4 copy.19
  154.2 0.0 collective-permute-done.4
  154.2 0.0 copy-done.1
  154.2 6.5 %fusion.26 = f32[8,512,640]{2,1,0:T(8,128)} fusion(bf16[64,8,8,128]{3,2,1,0:T(8,128)(2,1)S(1)} %copy-done.1, bf16[128,1024]{1,0:T(8,128)(2,1)} %collective-permute-done.4, bf16[512,1024]{1,0:T(8,128)(2,1)S(1)} %get-tuple-element.14), kind=kOutput, calls=%fused_computation.32 | convolution fusion | flops 673710080 | bytes 12845056 | tf_op jit(solution)/shard_map/qhd,khd->hqk/dot_general | solution.py:78
  160.8 0.0 copy-done.3
  160.8 16.0 %fusion.42 = (f32[8,512]{1,0:T(8,128)S(1)}, f32[8,512,640]{2,1,0:T(8,128)}) fusion(f32[8,512,640]{2,1,0:T(8,128)} %fusion.26, pred[512,640]{1,0:T(8,128)(4,1)S(1)} %copy-done.3), kind=kOutput, calls=%fused_computation.63 | output fusion | flops 15729279 | bytes 21315584 | tf_op jit(solution)/shard_map/sub | solution.py:84
  176.8 0.0 copy-done.2
  176.8 6.0 %fusion.25 = bf16[8,128,512]{2,1,0:T(8,128)(2,1)S(1)} fusion(bf16[640,8,128]{0,2,1:T(8,128)(2,1)S(1)} %bitcast.51, f32[8,512,640]{2,1,0:T(8,128)} %get-tuple-element.18, f32[8,512]{1,0:T(8,128)S(1)} %get-tuple-element.17), kind=kOutput, calls=%fused_computation.31 | convolution fusion | flops 676855808 | bytes 12861440 | tf_op jit(solution)/shard_map/hqk,khd->qhd/dot_general | solution.py:89
  182.8 1.8 collective-permute-start.6
  184.6 0.0 copy-done.4
  184.6 1.3 reduce-window.6
  186.0 0.2 slice_reduce_fusion
  186.2 0.1 fusion.37
  186.3 0.0 copy-start.9
  186.3 10.2 %all-gather.5.cloned.1.call-done = bf16[3200,1024]{1,0:T(8,128)(2,1)} async-done(((bf16[200,1024]{1,0:T(8,128)(2,1)}), bf16[3200,1024]{1,0:T(8,128)(2,1)}) %all-gather.5.cloned.1.call-update) | async-done | bytes 6553616 | tf_op jit(solution)/shard_map/all_gather | solution.py:50
  196.6 5.0 %fusion.17 = bf16[512,1600]{0,1:T(8,128)(2,1)} fusion(bf16[512,1024]{0,1:T(8,128)(2,1)S(1)} %bitcast.59, bf16[3200,1024]{1,0:T(8,128)(2,1)} %all-gather.5.cloned.1.call-done), kind=kOutput, calls=%fused_computation.23 | convolution fusion | flops 1678540800 | bytes 5963776 | tf_op jit(solution)/shard_map/dot_general | solution.py:94
  201.6 6.6 %collective-permute-done.6 = bf16[512,1024]{0,1:T(8,128)(2,1)S(1)} collective-permute-done((bf16[512,1024]{0,1:T(8,128)(2,1)S(1)}, bf16[512,1024]{0,1:T(8,128)(2,1)S(1)}, u32[]{:S(2)}, u32[]{:S(2)}) %collective-permute-start.6) | collective-permute-done | bytes 1048608 | tf_op jit(solution)/shard_map/ppermute | solution.py:19
  208.2 8.5 %convolution_convert_fusion = bf16[1024,1600]{0,1:T(8,128)(2,1)} fusion(s32[512]{0:T(512)S(1)} %multiply_add_fusion, bf16[512,1600]{0,1:T(8,128)(2,1)} %fusion.17, bf16[512,1600]{0,1:T(8,128)(2,1)} %param.8, bf16[512,1024]{0,1:T(8,128)(2,1)S(1)} %collective-permute-done.6, bf16[3200,1024]{1,0:T(8,128)(2,1)} %all-gather.5.cloned.1.call-done, ...), kind=kOutput, calls=%fused_computation.14 | convolution fusion | flops 3364159488 | bytes 10887424 | tf_op jit(solution)/shard_map/dot_general | solution.py:110
  216.7 4.3 %copy.18 = bf16[1024,1600]{1,0:T(8,128)(2,1)S(1)} copy(bf16[1024,1600]{0,1:T(8,128)(2,1)} %convolution_convert_fusion) | data formatting | bytes 6553600 | tf_op jit(solution)/shard_map/convert_element_type | solution.py:110
  221.1 87.3 %all_to_all.5 = bf16[16,64,1600]{2,1,0:T(8,128)(2,1)S(1)} all-to-all(bf16[16,64,1600]{2,1,0:T(8,128)(2,1)S(1)} %bitcast.48), channel_id=1, replica_groups=mesh['group'=16,'tp'=2] {'group'}, dimensions={0} | all-to-all | bytes 6553600 | tf_op jit(solution)/shard_map/all_to_all | solution.py:112
  308.3 1.8 copy.38
  (17 shorter events, 0.2 us)
Async XLA Ops:
  6.5 107.8 %all-gather.3.cloned.1.call-start = ((), (), s32[]{:S(2)}) async-start(), calls=%async_computation.1 | async-start | bytes 20889600 | tf_op jit(solution)/shard_map/all_gather | solution.py:29
  9.0 187.6 %all-gather.5.cloned.1.call-start = ((), (), s32[]{:S(2)}) async-start(), calls=%async_computation.2 | async-start | bytes 6963200 | tf_op jit(solution)/shard_map/all_gather | solution.py:50
  9.0 38.0 %collective-permute-start = (bf16[512,1600]{0,1:T(8,128)(2,1)}, bf16[512,1600]{0,1:T(8,128)(2,1)}, u32[]{:S(2)}, u32[]{:S(2)}) collective-permute-start(bf16[512,1600]{0,1:T(8,128)(2,1)} %param.8), channel_id=1, source_target_pairs={{1,0},{0,1},{3,2},{2,3},{5,4},{4,5},{7,6},{6,7},{9,8},{8,9},{11,10... | collective-permute-start | bytes 4915208 | tf_op jit(solution)/shard_map/ppermute | solution.py:19
  11.3 37.2 %copy-start.8 = (bf16[1024,200]{0,1:T(8,128)(2,1)S(1)}, bf16[1024,200]{0,1:T(8,128)(2,1)}, u32[]{:S(2)}) copy-start(bf16[1024,200]{0,1:T(8,128)(2,1)} %param.12) | copy-start | bytes 1228804
  11.3 38.7 %copy-start.5 = (bf16[1600]{0:T(1024)(128)(2,1)S(1)}, bf16[1600]{0:T(1024)(128)(2,1)}, u32[]{:S(2)}) copy-start(bf16[1600]{0:T(1024)(128)(2,1)} %param.9) | copy-start | bytes 9604
  11.4 69.8 %copy-start.6 = (s32[512]{0:T(512)S(1)}, s32[512]{0:T(512)}, u32[]{:S(2)}) copy-start(s32[512]{0:T(512)} %param.14) | copy-start | bytes 6148
  11.4 72.2 %copy-start.7 = (f32[2,1024]{1,0:T(2,128)S(1)}, f32[2,1024]{1,0:T(2,128)}, u32[]{:S(2)}) copy-start(f32[2,1024]{1,0:T(2,128)} %param.11) | copy-start | bytes 24580
  48.6 1.4 collective-permute-start.5
  50.1 34.4 %collective-permute-start.1 = (bf16[1,1600]{1,0:T(2,128)(2,1)S(1)}, bf16[1,1600]{1,0:T(2,128)(2,1)S(1)}, u32[]{:S(2)}, u32[]{:S(2)}) collective-permute-start(bf16[1,1600]{1,0:T(2,128)(2,1)S(1)} %reshape.96), channel_id=1, source_target_pairs={{1,0},{0,1},{3,2},{2,3},{5,4},{4,5},{7,6},{6,7},{9,8},{8,9},{11,10... | collective-permute-start | bytes 9608 | tf_op jit(solution)/shard_map/ppermute | solution.py:19
  81.3 3.2 collective-permute-start.3
  128.6 2.7 copy-start
  128.8 22.9 %collective-permute-start.2 = (bf16[128,1024]{1,0:T(8,128)(2,1)S(1)}, bf16[128,1024]{1,0:T(8,128)(2,1)}, u32[]{:S(2)}, u32[]{:S(2)}) collective-permute-start(bf16[128,1024]{1,0:T(8,128)(2,1)S(1)} %constant_dynamic-slice_fusion.1), channel_id=1, source_target_pairs={{0,2},{2,0},{4,6},{6,4},{8,10},{10,8},{12,14},{14,12},{16,18},{18,... | collective-permute-start | bytes 786440 | tf_op jit(solution)/shard_map/ppermute | solution.py:14
  150.0 4.2 %collective-permute-start.4 = (bf16[128,1024]{1,0:T(8,128)(2,1)}, bf16[128,1024]{1,0:T(8,128)(2,1)}, u32[]{:S(2)}, u32[]{:S(2)}) collective-permute-start(bf16[128,1024]{1,0:T(8,128)(2,1)} %constant_dynamic-slice_fusion), channel_id=1, source_target_pairs={{0,2},{2,0},{4,6},{6,4},{8,10},{10,8},{12,14},{14,12},{16,18},{18,... | collective-permute-start | bytes 786440 | tf_op jit(solution)/shard_map/ppermute | solution.py:14
  152.8 1.5 copy-start.1
  154.2 6.5 %copy-start.3 = (pred[512,640]{1,0:T(8,128)(4,1)S(1)}, pred[512,640]{1,0:T(8,128)(4,1)}, u32[]{:S(2)}) copy-start(pred[512,640]{1,0:T(8,128)(4,1)} %broadcast_compare_fusion) | copy-start | bytes 983044
  160.8 16.0 %copy-start.2 = (bf16[640,1024]{0,1:T(8,128)(2,1)S(1)}, bf16[640,1024]{0,1:T(8,128)(2,1)}, u32[]{:S(2)}) copy-start(bf16[640,1024]{0,1:T(8,128)(2,1)} %copy.19) | copy-start | bytes 3932164
  176.8 7.8 %copy-start.4 = (s32[512,1]{0,1:T(1,128)S(1)}, s32[512,1]{0,1:T(1,128)}, u32[]{:S(2)}) copy-start(s32[512,1]{0,1:T(1,128)} %param.15) | copy-start | bytes 6148
  182.8 25.4 %collective-permute-start.6 = (bf16[512,1024]{0,1:T(8,128)(2,1)S(1)}, bf16[512,1024]{0,1:T(8,128)(2,1)S(1)}, u32[]{:S(2)}, u32[]{:S(2)}) collective-permute-start(bf16[512,1024]{0,1:T(8,128)(2,1)S(1)} %bitcast.58), channel_id=1, source_target_pairs={{1,0},{0,1},{3,2},{2,3},{5,4},{4,5},{7,6},{6,7},{9,8},{8,9},{11,10... | collective-permute-start | bytes 3145736 | tf_op jit(solution)/shard_map/ppermute | solution.py:19
  186.3 21.9 %copy-start.9 = (f32[1600]{0:T(1024)S(1)}, f32[1600]{0:T(1024)}, u32[]{:S(2)}) copy-start(f32[1600]{0:T(1024)} %param.13) | copy-start | bytes 19204
Sparse Core Ops, SparseCore 0:
  9.1 105.1 all-gather.2
  116.6 79.9 all-gather.4
where the time goes:
time: 317 us
  blocking collectives  102 us (32%)
  waiting for transfers between devices  80.1 us (25%)
  matrix products  40.3 us (13%)
  starting transfers between devices  39.9 us (13%)
  other arithmetic  24.4 us (8%)
  local copies, waits for them, and re-layouts  17 us (5%)
  between operations  13.6 us (4%)
    all_to_all x1, blocking collectives, shards(): lax.all_to_all(outbox, 'group', split_axis=0, concat_axis=0, tiled=True)  87.3 us
    ppermute x3, waiting for transfers between devices, from_next(): lax.ppermute(value, axis, [((i + 1) % count, i) for i in range(count)])  40.6 us
    ppermute x3, starting transfers between devices, from_next(): lax.ppermute(value, axis, [((i + 1) % count, i) for i in range(count)])  35.1 us
    all_gather x1, waiting for transfers between devices, shards(): lax.all_gather(w_qkv.reshape(w_qkv.shape[0], 3 * local_width), 'group', a...  28.8 us
    sub x1, other arithmetic, shards(): expo = jnp.exp(scores - top)  16 us
    psum x1, blocking collectives, shards(): lax.psum((jnp.sum(query * query, axis=-1), jnp.sum(key_rows * key_rows, a...  14.3 us
    dot_general x1, matrix products, shards(): qkv = jnp.dot(normed, w_all, preferred_element_type=jnp.float32)  14.3 us
    all_gather x1, waiting for transfers between devices, shards(): w_o = lax.all_gather(w_piece, 'group', axis=0, tiled=True)  10.2 us
  transfers between devices with their start and end apart: 9, of which 5 were waited for; matrix products, arithmetic and copies ran while one was open for 20% of the time, Pallas kernels for 0%

commit v1 on v0

--- a/solution.py
+++ b/solution.py
@@ -47,7 +47,16 @@
             to_g = (b - t) % tp_count * per + j
             pairs.append((g * tp_count + b, to_g * tp_count + t))
     w_piece = lax.ppermute(late_out.T, ("group", "tp"), pairs)
-    w_o = lax.all_gather(w_piece, "group", axis=0, tiled=True)
+    n_parts = jax.lax.psum(1, axis_name="group")
+    new = sorted(((ii, (ii + 1) % n_parts) for ii in range(n_parts)))
+    everything = w_piece
+    pile = [everything]
+    for u in [*range(1, n_parts)]:
+        everything = jax.lax.ppermute(everything, "group", perm=new)
+        pile.insert(0, everything)
+    left_arr = jnp.concatenate(pile, 0)
+    carry_in = jax.lax.axis_index("group") + 1
+    w_o = jnp.roll(left_arr, carry_in * w_piece.shape[0], 0)
     w_o = w_o.reshape(tp_count, feat_local, local_width)
     xwide = whole.astype(jnp.float32)
     stat = jnp.mean(xwide * xwide, axis=-1, keepdims=True)

time: 317 us -> 483 us (1.52)
  waiting for transfers between devices: 80.1 us -> 209 us
  local copies, waits for them, and re-layouts: 17 us -> 63.3 us
  blocking collectives: 102 us -> 89.7 us
    ppermute x0 -> x15, waiting for transfers between devices: none -> 161 us  [shards(): everything = jax.lax.ppermute(everything, 'group', perm=new)]
    unnamed x21 -> x106, local copies, waits for them, and re-layouts: 3.59 us -> 49.2 us
    all_gather x1, waiting for transfers between devices: 28.8 us -> 0.01 us  [shards(): lax.all_gather(w_qkv.reshape(w_qkv.shape[0], 3 * local_width), 'group', a...]
    ppermute x3, starting transfers between devices: 35.1 us -> 11.5 us  [from_next(): lax.ppermute(value, axis, [((i + 1) % count, i) for i in range(count)])]
    ppermute x3, starting transfers between devices: 3.36 us -> 18.9 us  [swapped(): return lax.ppermute(value, axis, pairs)]
    all_gather x1 -> x0, waiting for transfers between devices: 10.2 us -> none  [shards(): w_o = lax.all_gather(w_piece, 'group', axis=0, tiled=True)]
    ppermute x0 -> x15, starting transfers between devices: none -> 9.84 us  [shards(): everything = jax.lax.ppermute(everything, 'group', perm=new)]
    all_to_all x1, blocking collectives: 87.3 us -> 79.9 us  [shards(): lax.all_to_all(outbox, 'group', split_axis=0, concat_axis=0, tiled=True)]
  transfers between devices with their start and end apart: 9 -> 23, of which waited for: 5 -> 16; matrix products, arithmetic and copies ran while one was open for 20% -> 12% of each run, Pallas kernels for 0% -> 0%
where the time goes in v1:
time: 483 us
  waiting for transfers between devices  209 us (43%)
  blocking collectives  89.7 us (19%)
  local copies, waits for them, and re-layouts  63.3 us (13%)
  starting transfers between devices  41.9 us (9%)
  matrix products  40.9 us (8%)
  other arithmetic  23.6 us (5%)
  between operations  13.7 us (3%)
    ppermute x15, waiting for transfers between devices, shards(): everything = jax.lax.ppermute(everything, 'group', perm=new)  161 us
    all_to_all x1, blocking collectives, shards(): lax.all_to_all(outbox, 'group', split_axis=0, concat_axis=0, tiled=True)  79.9 us
    unnamed x106, local copies, waits for them, and re-layouts  49.2 us
    ppermute x3, waiting for transfers between devices, from_next(): lax.ppermute(value, axis, [((i + 1) % count, i) for i in range(count)])  47.9 us
    ppermute x3, starting transfers between devices, swapped(): return lax.ppermute(value, axis, pairs)  18.9 us
    sub x1, other arithmetic, shards(): expo = jnp.exp(scores - top)  15.5 us
    dot_general x1, matrix products, shards(): qkv = jnp.dot(normed, w_all, preferred_element_type=jnp.float32)  14.3 us
    ppermute x3, starting transfers between devices, from_next(): lax.ppermute(value, axis, [((i + 1) % count, i) for i in range(count)])  11.5 us
  transfers between devices with their start and end apart: 23, of which 16 were waited for; matrix products, arithmetic and copies ran while one was open for 12% of the time, Pallas kernels for 0%

profile of v1, /device:TPU:1, one launch (start us, length us, event | category | flops | bytes accessed | tf_op | source)
XLA Modules:
  0.0 482.5 jit_solution(7151782634676789641)
XLA Ops:
  6.6 2.4 copy.23
  9.0 2.1 collective-permute-start
  11.3 1.6 constant_dynamic-update-slice_fusion.33
  12.9 34.0 %collective-permute-done = bf16[512,1600]{0,1:T(8,128)(2,1)} collective-permute-done((bf16[512,1600]{0,1:T(8,128)(2,1)}, bf16[512,1600]{0,1:T(8,128)(2,1)}, u32[]{:S(2)}, u32[]{:S(2)}) %collective-permute-start) | collective-permute-done | bytes 1638432 | tf_op jit(solution)/shard_map/ppermute | solution.py:19
  47.0 1.6 constant_dynamic-update-slice_fusion.32
  48.6 1.7 collective-permute-start.5
  51.0 2.6 collective-permute-start.6
  53.7 13.6 %collective-permute-done.6 = bf16[200,1024]{1,0:T(8,128)(2,1)S(1)} collective-permute-done((bf16[200,1024]{1,0:T(8,128)(2,1)S(1)}, bf16[200,1024]{1,0:T(8,128)(2,1)S(1)}, u32[]{:S(2)}, u32[]{:S(2)}) %collective-permute-start.6) | collective-permute-done | bytes 409632 | tf_op jit(solution)/shard_map/ppermute | solution.py:55
  68.0 2.5 collective-permute-start.7
  70.5 32.5 %collective-permute-done.7 = bf16[200,1024]{1,0:T(8,128)(2,1)S(1)} collective-permute-done((bf16[200,1024]{1,0:T(8,128)(2,1)S(1)}, bf16[200,1024]{1,0:T(8,128)(2,1)S(1)}, u32[]{:S(2)}, u32[]{:S(2)}) %collective-permute-start.7) | collective-permute-done | bytes 409632 | tf_op jit(solution)/shard_map/ppermute | solution.py:55
  103.7 18.6 %collective-permute-done.8 = bf16[200,1024]{1,0:T(8,128)(2,1)S(1)} collective-permute-done((bf16[200,1024]{1,0:T(8,128)(2,1)S(1)}, bf16[200,1024]{1,0:T(8,128)(2,1)S(1)}, u32[]{:S(2)}, u32[]{:S(2)}) %collective-permute-start.8) | collective-permute-done | bytes 409632 | tf_op jit(solution)/shard_map/ppermute | solution.py:55
  123.1 10.1 %collective-permute-done.9 = bf16[200,1024]{1,0:T(8,128)(2,1)S(1)} collective-permute-done((bf16[200,1024]{1,0:T(8,128)(2,1)S(1)}, bf16[200,1024]{1,0:T(8,128)(2,1)S(1)}, u32[]{:S(2)}, u32[]{:S(2)}) %collective-permute-start.9) | collective-permute-done | bytes 409632 | tf_op jit(solution)/shard_map/ppermute | solution.py:55
  134.0 10.1 %collective-permute-done.10 = bf16[200,1024]{1,0:T(8,128)(2,1)S(1)} collective-permute-done((bf16[200,1024]{1,0:T(8,128)(2,1)S(1)}, bf16[200,1024]{1,0:T(8,128)(2,1)S(1)}, u32[]{:S(2)}, u32[]{:S(2)}) %collective-permute-start.10) | collective-permute-done | bytes 409632 | tf_op jit(solution)/shard_map/ppermute | solution.py:55
  144.8 10.1 %collective-permute-done.11 = bf16[200,1024]{1,0:T(8,128)(2,1)S(1)} collective-permute-done((bf16[200,1024]{1,0:T(8,128)(2,1)S(1)}, bf16[200,1024]{1,0:T(8,128)(2,1)S(1)}, u32[]{:S(2)}, u32[]{:S(2)}) %collective-permute-start.11) | collective-permute-done | bytes 409632 | tf_op jit(solution)/shard_map/ppermute | solution.py:55
  155.6 10.1 %collective-permute-done.12 = bf16[200,1024]{1,0:T(8,128)(2,1)S(1)} collective-permute-done((bf16[200,1024]{1,0:T(8,128)(2,1)S(1)}, bf16[200,1024]{1,0:T(8,128)(2,1)S(1)}, u32[]{:S(2)}, u32[]{:S(2)}) %collective-permute-start.12) | collective-permute-done | bytes 409632 | tf_op jit(solution)/shard_map/ppermute | solution.py:55
  166.5 10.1 %collective-permute-done.13 = bf16[200,1024]{1,0:T(8,128)(2,1)S(1)} collective-permute-done((bf16[200,1024]{1,0:T(8,128)(2,1)S(1)}, bf16[200,1024]{1,0:T(8,128)(2,1)S(1)}, u32[]{:S(2)}, u32[]{:S(2)}) %collective-permute-start.13) | collective-permute-done | bytes 409632 | tf_op jit(solution)/shard_map/ppermute | solution.py:55
  177.3 10.1 %collective-permute-done.14 = bf16[200,1024]{1,0:T(8,128)(2,1)S(1)} collective-permute-done((bf16[200,1024]{1,0:T(8,128)(2,1)S(1)}, bf16[200,1024]{1,0:T(8,128)(2,1)S(1)}, u32[]{:S(2)}, u32[]{:S(2)}) %collective-permute-start.14) | collective-permute-done | bytes 409632 | tf_op jit(solution)/shard_map/ppermute | solution.py:55
  188.2 10.1 %collective-permute-done.15 = bf16[200,1024]{1,0:T(8,128)(2,1)S(1)} collective-permute-done((bf16[200,1024]{1,0:T(8,128)(2,1)S(1)}, bf16[200,1024]{1,0:T(8,128)(2,1)S(1)}, u32[]{:S(2)}, u32[]{:S(2)}) %collective-permute-start.15) | collective-permute-done | bytes 409632 | tf_op jit(solution)/shard_map/ppermute | solution.py:55
  199.0 10.2 %collective-permute-done.16 = bf16[200,1024]{1,0:T(8,128)(2,1)} collective-permute-done((bf16[200,1024]{1,0:T(8,128)(2,1)S(1)}, bf16[200,1024]{1,0:T(8,128)(2,1)}, u32[]{:S(2)}, u32[]{:S(2)}) %collective-permute-start.16) | collective-permute-done | bytes 409632 | tf_op jit(solution)/shard_map/ppermute | solution.py:55
  209.2 7.6 %collective-permute-start.1 = (bf16[1,1600]{1,0:T(2,128)(2,1)S(1)}, bf16[1,1600]{1,0:T(2,128)(2,1)S(1)}, u32[]{:S(2)}, u32[]{:S(2)}) collective-permute-start(bf16[1,1600]{1,0:T(2,128)(2,1)S(1)} %reshape.96), channel_id=1, source_target_pairs={{1,0},{0,1},{3,2},{2,3},{5,4},{4,5},{7,6},{6,7},{9,8},{8,9},{11,10... | collective-permute-start | bytes 9608 | tf_op jit(solution)/shard_map/ppermute | solution.py:19
  216.9 9.1 %collective-permute-start.3 = (s32[128]{0:T(128)S(1)}, s32[128]{0:T(128)S(1)}, u32[]{:S(2)}, u32[]{:S(2)}) collective-permute-start(s32[128]{0:T(128)S(1)} %dynamic_slice.14), channel_id=1, source_target_pairs={{0,2},{2,0},{4,6},{6,4},{8,10},{10,8},{12,14},{14,12},{16,18},{18,... | collective-permute-start | bytes 1544 | tf_op jit(solution)/shard_map/ppermute | solution.py:14
  226.0 1.2 reduce-window.6
  227.6 4.8 %collective-permute-done.18 = bf16[200,1024]{1,0:T(8,128)(2,1)} collective-permute-done((bf16[200,1024]{1,0:T(8,128)(2,1)}, bf16[200,1024]{1,0:T(8,128)(2,1)}, u32[]{:S(2)}, u32[]{:S(2)}) %collective-permute-start.18) | collective-permute-done | bytes 409632 | tf_op jit(solution)/shard_map/ppermute | solution.py:55
  232.4 2.5 collective-permute-start.19
  235.1 1.0 broadcast_compare_fusion
  236.5 3.9 collective-permute-done.19
  240.4 2.2 collective-permute-start.20
  243.3 7.3 %collective-permute-done.20 = bf16[200,1024]{1,0:T(8,128)(2,1)S(1)} collective-permute-done((bf16[200,1024]{1,0:T(8,128)(2,1)}, bf16[200,1024]{1,0:T(8,128)(2,1)S(1)}, u32[]{:S(2)}, u32[]{:S(2)}) %collective-permute-start.20) | collective-permute-done | bytes 409632 | tf_op jit(solution)/shard_map/ppermute | solution.py:55
  250.7 0.8 constant_dynamic-update-slice_fusion.31
  251.5 1.8 constant_dynamic-update-slice_fusion.30
  253.2 1.8 constant_dynamic-update-slice_fusion.29
  255.0 1.8 constant_dynamic-update-slice_fusion.28
  256.8 1.8 constant_dynamic-update-slice_fusion.27
  258.6 1.8 constant_dynamic-update-slice_fusion.26
  260.4 1.8 constant_dynamic-update-slice_fusion.25
  262.2 1.8 constant_dynamic-update-slice_fusion.24
  264.0 1.8 constant_dynamic-update-slice_fusion.23
  267.3 0.8 constant_dynamic-update-slice_fusion.20
  268.1 0.8 constant_dynamic-update-slice_fusion.19
  268.9 0.8 constant_dynamic-update-slice_fusion.18
  269.8 0.8 constant_dynamic-update-slice_fusion.17
  272.1 1.8 constant_dynamic-update-slice_fusion.14
  274.0 1.8 constant_dynamic-update-slice_fusion.13
  275.7 1.8 constant_dynamic-update-slice_fusion.12
  277.5 1.8 constant_dynamic-update-slice_fusion.11
  280.9 0.8 constant_dynamic-update-slice_fusion.8
  282.5 14.3 %fusion.9 = f32[512,3072]{1,0:T(8,128)S(1)} fusion(bf16[3200,3072]{1,0:T(8,128)(2,1)} %all-gather.2.cloned.1.call-done, bf16[512,3200]{0,1:T(8,128)(2,1)S(1)} %constant_dynamic-update-slice_fusion.32, f32[3200]{0:T(1024)S(1)} %mul.109, f32[512]{0:T(512)S(1)} %add_rsqrt_fusion.2), kind=kOutput, calls=%fused_computation.15 | convolution fusion | flops 10072883200 | bytes 29243904 | tf_op jit(solution)/shard_map/dot_general | solution.py:64
  297.0 2.4 copy-done
  299.8 8.9 %collective-permute-start.2 = (bf16[128,1024]{1,0:T(8,128)(2,1)S(1)}, bf16[128,1024]{1,0:T(8,128)(2,1)}, u32[]{:S(2)}, u32[]{:S(2)}) collective-permute-start(bf16[128,1024]{1,0:T(8,128)(2,1)S(1)} %constant_dynamic-slice_fusion.1), channel_id=1, source_target_pairs={{0,2},{2,0},{4,6},{6,4},{8,10},{10,8},{12,14},{14,12},{16,18},{18,... | collective-permute-start | bytes 786440 | tf_op jit(solution)/shard_map/ppermute | solution.py:14
  308.7 9.8 %all-reduce = (f32[512]{0:T(512)S(1)}, f32[512]{0:T(512)S(1)}) all-reduce(f32[512]{0:T(512)S(1)} %get-tuple-element.10, f32[512]{0:T(512)S(1)} %get-tuple-element.9), channel_id=1, replica_groups=mesh['group'=16,'tp'=2] {'tp'}, use_global_device_ids=true, to_apply=%region_7.8 | all-reduce | flops 1024 | bytes 8192 | tf_op jit(solution)/shard_map/psum | solution.py:68
  318.5 3.6 fusion.29
  322.9 0.9 collective-permute-start.4
  324.6 1.0 pad_maximum_fusion
  325.6 1.4 copy.19
  327.1 6.8 %fusion.26 = f32[8,512,640]{2,1,0:T(8,128)} fusion(bf16[64,8,8,128]{3,2,1,0:T(8,128)(2,1)} %get-tuple-element.13, bf16[128,1024]{1,0:T(8,128)(2,1)} %collective-permute-done.4, bf16[512,1024]{1,0:T(8,128)(2,1)S(1)} %get-tuple-element.14), kind=kOutput, calls=%fused_computation.32 | convolution fusion | flops 673710080 | bytes 12845056 | tf_op jit(solution)/shard_map/qhd,khd->hqk/dot_general | solution.py:87
  333.9 15.5 %fusion.45 = (f32[8,512]{1,0:T(8,128)S(1)}, f32[8,512,640]{2,1,0:T(8,128)}) fusion(f32[8,512,640]{2,1,0:T(8,128)} %fusion.26, pred[512,640]{1,0:T(8,128)(4,1)} %broadcast_compare_fusion), kind=kOutput, calls=%fused_computation.97 | output fusion | flops 15729279 | bytes 21315584 | tf_op jit(solution)/shard_map/sub | solution.py:93
  349.5 6.1 %fusion.25 = bf16[8,128,512]{2,1,0:T(8,128)(2,1)S(1)} fusion(bf16[640,8,128]{0,2,1:T(8,128)(2,1)S(1)} %bitcast.51, f32[8,512,640]{2,1,0:T(8,128)} %get-tuple-element.18, f32[8,512]{1,0:T(8,128)S(1)} %get-tuple-element.17), kind=kOutput, calls=%fused_computation.31 | convolution fusion | flops 676855808 | bytes 12861440 | tf_op jit(solution)/shard_map/hqk,khd->qhd/dot_general | solution.py:98
  355.5 1.8 collective-permute-start.21
  362.1 5.0 %fusion.17 = bf16[512,1600]{0,1:T(8,128)(2,1)} fusion(bf16[512,1024]{0,1:T(8,128)(2,1)S(1)} %bitcast.59, bf16[6400,1024]{1,0:T(8,128)(2,1)} %constant_dynamic-update-slice_fusion, s32[]{:T(128)S(6)} %select_n.54), kind=kOutput, calls=%fused_computation.23 | convolution fusion | flops 1678540800 | bytes 5963780 | tf_op jit(solution)/shard_map/dot_general | solution.py:103
  367.1 13.9 %collective-permute-done.21 = bf16[512,1024]{0,1:T(8,128)(2,1)} collective-permute-done((bf16[512,1024]{0,1:T(8,128)(2,1)S(1)}, bf16[512,1024]{0,1:T(8,128)(2,1)}, u32[]{:S(2)}, u32[]{:S(2)}) %collective-permute-start.21) | collective-permute-done | bytes 1048608 | tf_op jit(solution)/shard_map/ppermute | solution.py:19
  381.0 8.7 %convolution_convert_fusion = bf16[1024,1600]{0,1:T(8,128)(2,1)} fusion(s32[512]{0:T(512)S(1)} %multiply_add_fusion, bf16[512,1600]{0,1:T(8,128)(2,1)} %fusion.17, bf16[512,1600]{0,1:T(8,128)(2,1)S(1)} %copy-done.30, bf16[512,1024]{0,1:T(8,128)(2,1)} %collective-permute-done.21, bf16[6400,1024]{1,0:T(8,128)(2,1)} %constant_dynamic-update-slice_fusion, ...), kind=kOutput, calls=%fused_computation.14 | convolution fusion | flops 3364159488 | bytes 10887428 | tf_op jit(solution)/shard_map/dot_general | solution.py:119
  389.7 4.3 copy.18
  394.1 79.9 %all_to_all.5 = bf16[16,64,1600]{2,1,0:T(8,128)(2,1)S(1)} all-to-all(bf16[16,64,1600]{2,1,0:T(8,128)(2,1)S(1)} %bitcast.48), channel_id=1, replica_groups=mesh['group'=16,'tp'=2] {'group'}, dimensions={0} | all-to-all | bytes 6553600 | tf_op jit(solution)/shard_map/all_to_all | solution.py:121
  473.9 1.8 copy.69
  (130 shorter events, 22.8 us)
Async XLA Ops:
  6.5 202.7 %copy-start.33 = (bf16[1600]{0:T(1024)(128)(2,1)S(1)}, bf16[1600]{0:T(1024)(128)(2,1)}, u32[]{:S(2)}) copy-start(bf16[1600]{0:T(1024)(128)(2,1)} %param.9) | copy-start | bytes 9604
  6.5 210.3 %copy-start.34 = (s32[512]{0:T(512)S(1)}, s32[512]{0:T(512)}, u32[]{:S(2)}) copy-start(s32[512]{0:T(512)} %param.14) | copy-start | bytes 6148
  6.5 219.4 %copy-start.32 = (s32[512,1]{0,1:T(1,128)S(1)}, s32[512,1]{0,1:T(1,128)}, u32[]{:S(2)}) copy-start(s32[512,1]{0,1:T(1,128)} %param.15) | copy-start | bytes 6148
  6.5 221.0 %copy-start.35 = (f32[2,1024]{1,0:T(2,128)S(1)}, f32[2,1024]{1,0:T(2,128)}, u32[]{:S(2)}) copy-start(f32[2,1024]{1,0:T(2,128)} %param.11) | copy-start | bytes 24580
  6.5 275.9 %all-gather.2.cloned.1.call-start = ((), (), s32[]{:S(2)}) async-start(), calls=%async_computation.1 | async-start | bytes 20889600 | tf_op jit(solution)/shard_map/all_gather | solution.py:29
  9.0 38.0 %collective-permute-start = (bf16[512,1600]{0,1:T(8,128)(2,1)}, bf16[512,1600]{0,1:T(8,128)(2,1)}, u32[]{:S(2)}, u32[]{:S(2)}) collective-permute-start(bf16[512,1600]{0,1:T(8,128)(2,1)} %param.8), channel_id=1, source_target_pairs={{1,0},{0,1},{3,2},{2,3},{5,4},{4,5},{7,6},{6,7},{9,8},{8,9},{11,10... | collective-permute-start | bytes 4915208 | tf_op jit(solution)/shard_map/ppermute | solution.py:19
  48.6 1.7 collective-permute-start.5
  50.3 0.8 copy-start.1
  51.0 16.3 %collective-permute-start.6 = (bf16[200,1024]{1,0:T(8,128)(2,1)S(1)}, bf16[200,1024]{1,0:T(8,128)(2,1)S(1)}, u32[]{:S(2)}, u32[]{:S(2)}) collective-permute-start(bf16[200,1024]{1,0:T(8,128)(2,1)S(1)} %collective-permute-done.5), channel_id=1, source_target_pairs={{0,2},{2,4},{4,6},{6,8},{8,10},{10,12},{12,14},{14,16},{16,18},{18... | collective-permute-start | bytes 1228808 | tf_op jit(solution)/shard_map/ppermute | solution.py:55
  67.3 0.7 copy-start.4
  68.0 34.9 %collective-permute-start.7 = (bf16[200,1024]{1,0:T(8,128)(2,1)S(1)}, bf16[200,1024]{1,0:T(8,128)(2,1)S(1)}, u32[]{:S(2)}, u32[]{:S(2)}) collective-permute-start(bf16[200,1024]{1,0:T(8,128)(2,1)S(1)} %collective-permute-done.6), channel_id=1, source_target_pairs={{0,2},{2,4},{4,6},{6,8},{8,10},{10,12},{12,14},{14,16},{16,18},{18... | collective-permute-start | bytes 1228808 | tf_op jit(solution)/shard_map/ppermute | solution.py:55
  103.0 0.7 copy-start.7
  103.7 18.6 %collective-permute-start.8 = (bf16[200,1024]{1,0:T(8,128)(2,1)S(1)}, bf16[200,1024]{1,0:T(8,128)(2,1)S(1)}, u32[]{:S(2)}, u32[]{:S(2)}) collective-permute-start(bf16[200,1024]{1,0:T(8,128)(2,1)S(1)} %collective-permute-done.7), channel_id=1, source_target_pairs={{0,2},{2,4},{4,6},{6,8},{8,10},{10,12},{12,14},{14,16},{16,18},{18... | collective-permute-start | bytes 1228808 | tf_op jit(solution)/shard_map/ppermute | solution.py:55
  122.4 0.8 copy-start.10
  123.1 10.1 %collective-permute-start.9 = (bf16[200,1024]{1,0:T(8,128)(2,1)S(1)}, bf16[200,1024]{1,0:T(8,128)(2,1)S(1)}, u32[]{:S(2)}, u32[]{:S(2)}) collective-permute-start(bf16[200,1024]{1,0:T(8,128)(2,1)S(1)} %collective-permute-done.8), channel_id=1, source_target_pairs={{0,2},{2,4},{4,6},{6,8},{8,10},{10,12},{12,14},{14,16},{16,18},{18... | collective-permute-start | bytes 1228808 | tf_op jit(solution)/shard_map/ppermute | solution.py:55
  133.2 0.8 copy-start.13
  134.0 10.1 %collective-permute-start.10 = (bf16[200,1024]{1,0:T(8,128)(2,1)S(1)}, bf16[200,1024]{1,0:T(8,128)(2,1)S(1)}, u32[]{:S(2)}, u32[]{:S(2)}) collective-permute-start(bf16[200,1024]{1,0:T(8,128)(2,1)S(1)} %collective-permute-done.9), channel_id=1, source_target_pairs={{0,2},{2,4},{4,6},{6,8},{8,10},{10,12},{12,14},{14,16},{16,18},{18... | collective-permute-start | bytes 1228808 | tf_op jit(solution)/shard_map/ppermute | solution.py:55
  144.1 0.7 copy-start.16
  144.8 10.1 %collective-permute-start.11 = (bf16[200,1024]{1,0:T(8,128)(2,1)S(1)}, bf16[200,1024]{1,0:T(8,128)(2,1)S(1)}, u32[]{:S(2)}, u32[]{:S(2)}) collective-permute-start(bf16[200,1024]{1,0:T(8,128)(2,1)S(1)} %collective-permute-done.10), channel_id=1, source_target_pairs={{0,2},{2,4},{4,6},{6,8},{8,10},{10,12},{12,14},{14,16},{16,18},{18... | collective-permute-start | bytes 1228808 | tf_op jit(solution)/shard_map/ppermute | solution.py:55
  154.9 0.8 copy-start.19
  155.6 10.1 %collective-permute-start.12 = (bf16[200,1024]{1,0:T(8,128)(2,1)S(1)}, bf16[200,1024]{1,0:T(8,128)(2,1)S(1)}, u32[]{:S(2)}, u32[]{:S(2)}) collective-permute-start(bf16[200,1024]{1,0:T(8,128)(2,1)S(1)} %collective-permute-done.11), channel_id=1, source_target_pairs={{0,2},{2,4},{4,6},{6,8},{8,10},{10,12},{12,14},{14,16},{16,18},{18... | collective-permute-start | bytes 1228808 | tf_op jit(solution)/shard_map/ppermute | solution.py:55
  165.7 0.8 copy-start.22
  166.5 10.1 %collective-permute-start.13 = (bf16[200,1024]{1,0:T(8,128)(2,1)S(1)}, bf16[200,1024]{1,0:T(8,128)(2,1)S(1)}, u32[]{:S(2)}, u32[]{:S(2)}) collective-permute-start(bf16[200,1024]{1,0:T(8,128)(2,1)S(1)} %collective-permute-done.12), channel_id=1, source_target_pairs={{0,2},{2,4},{4,6},{6,8},{8,10},{10,12},{12,14},{14,16},{16,18},{18... | collective-permute-start | bytes 1228808 | tf_op jit(solution)/shard_map/ppermute | solution.py:55
  176.6 0.8 copy-start.24
  177.3 10.1 %collective-permute-start.14 = (bf16[200,1024]{1,0:T(8,128)(2,1)S(1)}, bf16[200,1024]{1,0:T(8,128)(2,1)S(1)}, u32[]{:S(2)}, u32[]{:S(2)}) collective-permute-start(bf16[200,1024]{1,0:T(8,128)(2,1)S(1)} %collective-permute-done.13), channel_id=1, source_target_pairs={{0,2},{2,4},{4,6},{6,8},{8,10},{10,12},{12,14},{14,16},{16,18},{18... | collective-permute-start | bytes 1228808 | tf_op jit(solution)/shard_map/ppermute | solution.py:55
  187.4 0.8 copy-start.26
  188.2 10.1 %collective-permute-start.15 = (bf16[200,1024]{1,0:T(8,128)(2,1)S(1)}, bf16[200,1024]{1,0:T(8,128)(2,1)S(1)}, u32[]{:S(2)}, u32[]{:S(2)}) collective-permute-start(bf16[200,1024]{1,0:T(8,128)(2,1)S(1)} %collective-permute-done.14), channel_id=1, source_target_pairs={{0,2},{2,4},{4,6},{6,8},{8,10},{10,12},{12,14},{14,16},{16,18},{18... | collective-permute-start | bytes 1228808 | tf_op jit(solution)/shard_map/ppermute | solution.py:55
  198.3 0.8 copy-start.28
  199.0 10.2 %collective-permute-start.16 = (bf16[200,1024]{1,0:T(8,128)(2,1)S(1)}, bf16[200,1024]{1,0:T(8,128)(2,1)}, u32[]{:S(2)}, u32[]{:S(2)}) collective-permute-start(bf16[200,1024]{1,0:T(8,128)(2,1)S(1)} %collective-permute-done.15), channel_id=1, source_target_pairs={{0,2},{2,4},{4,6},{6,8},{8,10},{10,12},{12,14},{14,16},{16,18},{18... | collective-permute-start | bytes 1228808 | tf_op jit(solution)/shard_map/ppermute | solution.py:55
  209.2 17.9 %collective-permute-start.17 = (bf16[200,1024]{1,0:T(8,128)(2,1)}, bf16[200,1024]{1,0:T(8,128)(2,1)}, u32[]{:S(2)}, u32[]{:S(2)}) collective-permute-start(bf16[200,1024]{1,0:T(8,128)(2,1)} %collective-permute-done.16), channel_id=1, source_target_pairs={{0,2},{2,4},{4,6},{6,8},{8,10},{10,12},{12,14},{14,16},{16,18},{18... | collective-permute-start | bytes 1228808 | tf_op jit(solution)/shard_map/ppermute | solution.py:55
  209.2 26.9 %collective-permute-start.1 = (bf16[1,1600]{1,0:T(2,128)(2,1)S(1)}, bf16[1,1600]{1,0:T(2,128)(2,1)S(1)}, u32[]{:S(2)}, u32[]{:S(2)}) collective-permute-start(bf16[1,1600]{1,0:T(2,128)(2,1)S(1)} %reshape.96), channel_id=1, source_target_pairs={{1,0},{0,1},{3,2},{2,3},{5,4},{4,5},{7,6},{6,7},{9,8},{8,9},{11,10... | collective-permute-start | bytes 9608 | tf_op jit(solution)/shard_map/ppermute | solution.py:19
  216.9 18.2 %collective-permute-start.3 = (s32[128]{0:T(128)S(1)}, s32[128]{0:T(128)S(1)}, u32[]{:S(2)}, u32[]{:S(2)}) collective-permute-start(s32[128]{0:T(128)S(1)} %dynamic_slice.14), channel_id=1, source_target_pairs={{0,2},{2,0},{4,6},{6,4},{8,10},{10,8},{12,14},{14,12},{16,18},{18,... | collective-permute-start | bytes 1544 | tf_op jit(solution)/shard_map/ppermute | solution.py:14
  227.1 5.3 %collective-permute-start.18 = (bf16[200,1024]{1,0:T(8,128)(2,1)}, bf16[200,1024]{1,0:T(8,128)(2,1)}, u32[]{:S(2)}, u32[]{:S(2)}) collective-permute-start(bf16[200,1024]{1,0:T(8,128)(2,1)} %collective-permute-done.17), channel_id=1, source_target_pairs={{0,2},{2,4},{4,6},{6,8},{8,10},{10,12},{12,14},{14,16},{16,18},{18... | collective-permute-start | bytes 1228808 | tf_op jit(solution)/shard_map/ppermute | solution.py:55
  232.4 8.0 %collective-permute-start.19 = (bf16[200,1024]{1,0:T(8,128)(2,1)}, bf16[200,1024]{1,0:T(8,128)(2,1)}, u32[]{:S(2)}, u32[]{:S(2)}) collective-permute-start(bf16[200,1024]{1,0:T(8,128)(2,1)} %collective-permute-done.18), channel_id=1, source_target_pairs={{0,2},{2,4},{4,6},{6,8},{8,10},{10,12},{12,14},{14,16},{16,18},{18... | collective-permute-start | bytes 1228808 | tf_op jit(solution)/shard_map/ppermute | solution.py:55
  236.4 29.3 %copy-start.20 = (bf16[200,1024]{1,0:T(8,128)(2,1)S(1)}, bf16[200,1024]{1,0:T(8,128)(2,1)}, u32[]{:S(2)}) copy-start(bf16[200,1024]{1,0:T(8,128)(2,1)} %copy-done.19) | copy-start | bytes 1228804
  236.4 30.1 %copy-start.17 = (bf16[200,1024]{1,0:T(8,128)(2,1)S(1)}, bf16[200,1024]{1,0:T(8,128)(2,1)}, u32[]{:S(2)}) copy-start(bf16[200,1024]{1,0:T(8,128)(2,1)} %copy-done.16) | copy-start | bytes 1228804
  236.4 30.9 %copy-start.14 = (bf16[200,1024]{1,0:T(8,128)(2,1)S(1)}, bf16[200,1024]{1,0:T(8,128)(2,1)}, u32[]{:S(2)}) copy-start(bf16[200,1024]{1,0:T(8,128)(2,1)} %copy-done.13) | copy-start | bytes 1228804
  236.4 31.7 %copy-start.11 = (bf16[200,1024]{1,0:T(8,128)(2,1)S(1)}, bf16[200,1024]{1,0:T(8,128)(2,1)}, u32[]{:S(2)}) copy-start(bf16[200,1024]{1,0:T(8,128)(2,1)} %copy-done.10) | copy-start | bytes 1228804
  236.5 32.5 %copy-start.8 = (bf16[200,1024]{1,0:T(8,128)(2,1)S(1)}, bf16[200,1024]{1,0:T(8,128)(2,1)}, u32[]{:S(2)}) copy-start(bf16[200,1024]{1,0:T(8,128)(2,1)} %copy-done.7) | copy-start | bytes 1228804
  236.5 33.3 %copy-start.5 = (bf16[200,1024]{1,0:T(8,128)(2,1)S(1)}, bf16[200,1024]{1,0:T(8,128)(2,1)}, u32[]{:S(2)}) copy-start(bf16[200,1024]{1,0:T(8,128)(2,1)} %copy-done.4) | copy-start | bytes 1228804
  236.5 34.1 %copy-start.2 = (bf16[200,1024]{1,0:T(8,128)(2,1)S(1)}, bf16[200,1024]{1,0:T(8,128)(2,1)}, u32[]{:S(2)}) copy-start(bf16[200,1024]{1,0:T(8,128)(2,1)} %copy-done.1) | copy-start | bytes 1228804
  236.5 42.8 %copy-start.29 = (bf16[200,1024]{1,0:T(8,128)(2,1)S(1)}, bf16[200,1024]{1,0:T(8,128)(2,1)}, u32[]{:S(2)}) copy-start(bf16[200,1024]{1,0:T(8,128)(2,1)} %copy-done.28) | copy-start | bytes 1228804
  236.5 43.6 %copy-start.27 = (bf16[200,1024]{1,0:T(8,128)(2,1)S(1)}, bf16[200,1024]{1,0:T(8,128)(2,1)}, u32[]{:S(2)}) copy-start(bf16[200,1024]{1,0:T(8,128)(2,1)} %copy-done.26) | copy-start | bytes 1228804
  236.5 44.4 %copy-start.25 = (bf16[200,1024]{1,0:T(8,128)(2,1)S(1)}, bf16[200,1024]{1,0:T(8,128)(2,1)}, u32[]{:S(2)}) copy-start(bf16[200,1024]{1,0:T(8,128)(2,1)} %copy-done.24) | copy-start | bytes 1228804
  240.4 10.3 %collective-permute-start.20 = (bf16[200,1024]{1,0:T(8,128)(2,1)}, bf16[200,1024]{1,0:T(8,128)(2,1)S(1)}, u32[]{:S(2)}, u32[]{:S(2)}) collective-permute-start(bf16[200,1024]{1,0:T(8,128)(2,1)} %collective-permute-done.19), channel_id=1, source_target_pairs={{0,2},{2,4},{4,6},{6,8},{8,10},{10,12},{12,14},{14,16},{16,18},{18... | collective-permute-start | bytes 1228808 | tf_op jit(solution)/shard_map/ppermute | solution.py:55
  243.3 38.4 %copy-start.23 = (bf16[200,1024]{1,0:T(8,128)(2,1)S(1)}, bf16[200,1024]{1,0:T(8,128)(2,1)}, u32[]{:S(2)}) copy-start(bf16[200,1024]{1,0:T(8,128)(2,1)} %copy-done.22) | copy-start | bytes 1228804
  296.8 2.6 copy-start
  296.8 27.0 %copy-start.21 = (bf16[200,1024]{1,0:T(8,128)(2,1)S(1)}, bf16[200,1024]{1,0:T(8,128)(2,1)}, u32[]{:S(2)}) copy-start(bf16[200,1024]{1,0:T(8,128)(2,1)} %copy-done.19) | copy-start | bytes 1228804
  299.8 24.7 %collective-permute-start.2 = (bf16[128,1024]{1,0:T(8,128)(2,1)S(1)}, bf16[128,1024]{1,0:T(8,128)(2,1)}, u32[]{:S(2)}, u32[]{:S(2)}) collective-permute-start(bf16[128,1024]{1,0:T(8,128)(2,1)S(1)} %constant_dynamic-slice_fusion.1), channel_id=1, source_target_pairs={{0,2},{2,0},{4,6},{6,4},{8,10},{10,8},{12,14},{14,12},{16,18},{18,... | collective-permute-start | bytes 786440 | tf_op jit(solution)/shard_map/ppermute | solution.py:14
  322.9 4.2 collective-permute-start.4
  333.9 15.5 %copy-start.31 = (bf16[640,1024]{0,1:T(8,128)(2,1)S(1)}, bf16[640,1024]{0,1:T(8,128)(2,1)}, u32[]{:S(2)}) copy-start(bf16[640,1024]{0,1:T(8,128)(2,1)} %copy.19) | copy-start | bytes 3932164
  349.4 8.0 %copy-start.18 = (bf16[200,1024]{1,0:T(8,128)(2,1)S(1)}, bf16[200,1024]{1,0:T(8,128)(2,1)}, u32[]{:S(2)}) copy-start(bf16[200,1024]{1,0:T(8,128)(2,1)} %copy-done.16) | copy-start | bytes 1228804
  349.4 8.8 %copy-start.15 = (bf16[200,1024]{1,0:T(8,128)(2,1)S(1)}, bf16[200,1024]{1,0:T(8,128)(2,1)}, u32[]{:S(2)}) copy-start(bf16[200,1024]{1,0:T(8,128)(2,1)} %copy-done.13) | copy-start | bytes 1228804
  349.4 9.5 %copy-start.12 = (bf16[200,1024]{1,0:T(8,128)(2,1)S(1)}, bf16[200,1024]{1,0:T(8,128)(2,1)}, u32[]{:S(2)}) copy-start(bf16[200,1024]{1,0:T(8,128)(2,1)} %copy-done.10) | copy-start | bytes 1228804
  349.4 10.3 %copy-start.9 = (bf16[200,1024]{1,0:T(8,128)(2,1)S(1)}, bf16[200,1024]{1,0:T(8,128)(2,1)}, u32[]{:S(2)}) copy-start(bf16[200,1024]{1,0:T(8,128)(2,1)} %copy-done.7) | copy-start | bytes 1228804
  349.4 11.1 %copy-start.6 = (bf16[200,1024]{1,0:T(8,128)(2,1)S(1)}, bf16[200,1024]{1,0:T(8,128)(2,1)}, u32[]{:S(2)}) copy-start(bf16[200,1024]{1,0:T(8,128)(2,1)} %copy-done.4) | copy-start | bytes 1228804
  349.4 11.9 %copy-start.3 = (bf16[200,1024]{1,0:T(8,128)(2,1)S(1)}, bf16[200,1024]{1,0:T(8,128)(2,1)}, u32[]{:S(2)}) copy-start(bf16[200,1024]{1,0:T(8,128)(2,1)} %copy-done.1) | copy-start | bytes 1228804
  355.5 25.5 %copy-start.30 = (bf16[512,1600]{0,1:T(8,128)(2,1)S(1)}, bf16[512,1600]{0,1:T(8,128)(2,1)}, u32[]{:S(2)}) copy-start(bf16[512,1600]{0,1:T(8,128)(2,1)} %param.8) | copy-start | bytes 4915204
  355.5 25.5 %copy-start.36 = (f32[1600]{0:T(1024)S(1)}, f32[1600]{0:T(1024)}, u32[]{:S(2)}) copy-start(f32[1600]{0:T(1024)} %param.13) | copy-start | bytes 19204
  355.5 25.5 %collective-permute-start.21 = (bf16[512,1024]{0,1:T(8,128)(2,1)S(1)}, bf16[512,1024]{0,1:T(8,128)(2,1)}, u32[]{:S(2)}, u32[]{:S(2)}) collective-permute-start(bf16[512,1024]{0,1:T(8,128)(2,1)S(1)} %bitcast.58), channel_id=1, source_target_pairs={{1,0},{0,1},{3,2},{2,3},{5,4},{4,5},{7,6},{6,7},{9,8},{8,9},{11,10... | collective-permute-start | bytes 3145736 | tf_op jit(solution)/shard_map/ppermute | solution.py:19
Sparse Core Ops, SparseCore 0:
  9.1 114.0 all-gather.1
